TPU v7x, 32 devices: a whole 2x2x4 slice. The times are simulated.
32 devices in a mesh: groups: 2 (over x), src: 16 (over z, y, core).
Axes of the slice: x: 2, y: 2, z: 4, core: 2. Of those that a mesh axis runs over, the one named last changes fastest.
Arguments:
- eigenvectors: bfloat16 [32, 2, 3, 16, 8, 4, 128], P('groups', None, None, 'src'), parts along dimension 0, may hold values from -0.71875 to 0.71875
- gauge_links: bfloat16 [32, 2, 2, 3, 3, 16, 8, 4], P('groups', None, None, None, None, 'src'), parts along dimension 0, may hold values from -2.5 to 2.5
- hop_path: int32 [4], P('groups'), parts along dimension 0, may hold values from 0 to 3, as said below
- spin_perm: int32 [4, 4], P('groups'), parts along dimension 0, may hold values from 0 to 3, each once within a row
- spin_phase: int32 [4, 4], P('groups'), parts along dimension 0, may hold values from 0 to 3
- perambulators: bfloat16 [32, 2, 512, 512], P('groups', None, 'src'), parts along dimension 0, may hold values from -0.1875 to 0.1875
- owned_times: int32 [32, 2], P('groups'), parts along dimension 0, may hold values from -1 to 15, as said below
Outputs:
- insertions: bfloat16 [64, 2, 2, 512, 512], P(('groups', 'src')), parts along dimension 0
There are 2 independent parts, one for each index of `groups`. A program takes and returns all parts, laid end to end along the dimension named above; each array names one. Nothing has to cross between parts.
Inputs may be any that keep to these rules, and one draw needn't show every extreme that they name: `hop_path`: codes 0, 1, 2, 3 stand for +y, -y, +z, -z; the 2 codes of the path are all different. `spin_perm`: each row is a permutation of the 4 spins. `owned_times`: every sink time 0 to 15 appears exactly once; a row lists its times first and then -1; a row lists at most 2 times, and some row exactly 2.
All inputs are finite; a program needn't handle non-finite values.
Results may differ from a plain program's by a relative error of at most 0.0058.
Values may be sent and summed in bfloat16 or wider, within the bound.
A program may use at most 128 MiB of HBM per device.

v0:
```python
import jax
import jax.numpy as jnp
from jax import lax
from jax.sharding import PartitionSpec as P


def adjoint(matrix):
    return jnp.stack([jnp.swapaxes(matrix[:, 0], 1, 2), -jnp.swapaxes(matrix[:, 1], 1, 2)], 1)


def plus_z(field, axis, zpos, side_z):
    return jnp.where(
        zpos == side_z - 1, jnp.roll(field, side_z - 1, axis), jnp.roll(field, -1, axis)
    )


def minus_z(field, axis, zpos, side_z):
    return jnp.where(zpos == 0, jnp.roll(field, 1 - side_z, axis), jnp.roll(field, 1, axis))


def displace(vectors, gauge_links, direction, side_z):
    merged = vectors.shape[4]
    zvec = (jnp.arange(merged) % side_z)[:, None]
    zlink = jnp.arange(merged) % side_z
    forward_y = gauge_links[:, 0]
    forward_z = gauge_links[:, 1]

    def case_up_y(field):
        return (forward_y, jnp.roll(field, -side_z, 4))

    def case_down_y(field):
        return (adjoint(jnp.roll(forward_y, side_z, 5)), jnp.roll(field, side_z, 4))

    def case_up_z(field):
        return (forward_z, plus_z(field, 4, zvec, side_z))

    def case_down_z(field):
        return (adjoint(minus_z(forward_z, 5, zlink, side_z)), minus_z(field, 4, zvec, side_z))

    link_pick, moved = lax.switch(
        direction, [case_up_y, case_down_y, case_up_z, case_down_z], vectors
    )
    link_re = link_pick[:, 0].astype(jnp.float32)
    link_im = link_pick[:, 1].astype(jnp.float32)
    moved_re = moved[:, 0].astype(jnp.float32)
    moved_im = moved[:, 1].astype(jnp.float32)
    real_rows = []
    imag_rows = []
    for colour in range(3):
        real_sum = jnp.zeros(moved_re[:, 0].shape, jnp.float32)
        imag_sum = jnp.zeros(moved_re[:, 0].shape, jnp.float32)
        for inner in range(3):
            coeff_re = link_re[:, colour, inner][..., None]
            coeff_im = link_im[:, colour, inner][..., None]
            real_sum = real_sum + coeff_re * moved_re[:, inner] - coeff_im * moved_im[:, inner]
            imag_sum = imag_sum + coeff_re * moved_im[:, inner] + coeff_im * moved_re[:, inner]
        real_rows.append(real_sum)
        imag_rows.append(imag_sum)
    return jnp.stack([jnp.stack(real_rows, 1), jnp.stack(imag_rows, 1)], 1).astype(jnp.bfloat16)


def correlations(eigen_merged, links_merged, hop_path, side_z):
    shifted = eigen_merged
    for hop_index in range(hop_path.shape[0]):
        shifted = displace(shifted, links_merged, hop_path[hop_index], side_z)
    time_count = eigen_merged.shape[0]
    eigen_width = eigen_merged.shape[-1]
    eigen_rows = eigen_merged.reshape(time_count, 2, -1, eigen_width)
    moved_rows = shifted.reshape(time_count, 2, -1, eigen_width)
    products = jnp.einsum(
        "tkra,tjrb->tkjab", eigen_rows, moved_rows, preferred_element_type=jnp.float32
    )
    return jnp.stack(
        [products[:, 0, 0] + products[:, 1, 1], products[:, 0, 1] - products[:, 1, 0]], 1
    )


def triple(stored, elemental, spin_perm, phase_re, phase_im):
    order = stored.shape[1]
    eigen_width = elemental.shape[1]
    spin_count = order // eigen_width
    group_count = spin_perm.shape[0]
    columns = stored.reshape(2, order, spin_count, eigen_width)
    permuted = jnp.take(columns, spin_perm, axis=2)
    products = jnp.einsum(
        "kab,jdgsb->kjgdsa", elemental, permuted, preferred_element_type=jnp.float32
    )
    real_part = products[0, 0] - products[1, 1]
    imag_part = products[0, 1] + products[1, 0]
    scale_re = phase_re[:, None, :, None]
    scale_im = phase_im[:, None, :, None]
    inserted = jnp.stack(
        [scale_re * real_part - scale_im * imag_part, scale_re * imag_part + scale_im * real_part],
        0,
    )
    inserted = inserted.reshape(2, group_count, order, order).astype(jnp.bfloat16)
    outer = jnp.einsum("kcr,jgdr->kjgcd", stored, inserted, preferred_element_type=jnp.float32)
    return jnp.stack([outer[0, 0] + outer[1, 1], outer[0, 1] - outer[1, 0]], 1)


def shards(eigenvectors, gauge_links, hop_path, spin_perm, spin_phase, perambulators, owned_times):
    time_count = eigenvectors.shape[0]
    plane_local = eigenvectors.shape[3]
    side_y = eigenvectors.shape[4]
    side_z = eigenvectors.shape[5]
    eigen_width = eigenvectors.shape[6]
    slot_count = owned_times.shape[1]
    eigen_merged = eigenvectors.reshape(time_count, 2, 3, plane_local, side_y * side_z, eigen_width)
    links_merged = gauge_links.reshape(time_count, 2, 2, 3, 3, plane_local, side_y * side_z)
    my_times = lax.dynamic_index_in_dim(owned_times, lax.axis_index("src"), 0, keepdims=False)
    listed = jnp.clip(owned_times.reshape(-1), 0, time_count - 1)
    partial_value = correlations(eigen_merged, links_merged, hop_path, side_z)
    outbound = jnp.take(partial_value, listed, axis=0)
    elemental = lax.psum_scatter(outbound, "src", scatter_dimension=0, tiled=True).astype(
        jnp.bfloat16
    )
    outgoing = jnp.take(perambulators, listed, axis=0)
    blocks = lax.all_to_all(outgoing, "src", split_axis=0, concat_axis=2, tiled=True)
    phase_re = (spin_phase == 0).astype(jnp.float32) - (spin_phase == 2).astype(jnp.float32)
    phase_im = (spin_phase == 1).astype(jnp.float32) - (spin_phase == 3).astype(jnp.float32)
    results = []
    for slot_index in range(slot_count):
        single = triple(blocks[slot_index], elemental[slot_index], spin_perm, phase_re, phase_im)
        filled = my_times[slot_index] >= 0
        results.append(jnp.where(filled, single, jnp.zeros_like(single)).astype(jnp.bfloat16))
    return jnp.stack(results, 0)


def solution(mesh):
    in_specs = (
        P("groups", None, None, "src", None, None, None),
        P("groups", None, None, None, None, "src", None, None),
        P("groups"),
        P("groups", None),
        P("groups", None),
        P("groups", None, "src", None),
        P("groups", None),
    )
    out_specs = P(("groups", "src"), None, None, None, None)
    return jax.shard_map(shards, mesh=mesh, in_specs=in_specs, out_specs=out_specs, check_vma=False)
```

profile of v0, /device:TPU:0, one launch (start us, length us, event | category | flops | bytes accessed | tf_op | source)
XLA Modules:
  0.0 178.9 jit_solution(16745457774663295989)
XLA Ops:
  7.0 0.6 and_select_fusion
  7.6 1.0 fusion.69
  8.6 0.7 copy.147
  9.4 1.3 fusion.75
  11.3 2.7 %conditional.2 = (bf16[16,2,3,3,1,32]{5,2,3,0,4,1:T(4,128)(2,1)}, f32[16,3,1,32,128]{4,3,1,0,2:T(8,128)S(1)}, f32[16,3,1,32,128]{4,3,1,0,2:T(8,128)S(1)}) conditional(s32[]{:T(128)} %bitcast.9, (bf16[16,2,3,1,32,128]{5,4,3,2,1,0:T(8,128)(2,1)}, bf16[16,2,3,3,1,32]{0,5,3,2,1,4:T(8,128)(2,1)S(1)}) %tuple.318, ...), branch_computations={%region_0.2_spmd.clone.clone, %region_1.3_spmd.clone.clone, %regio... | conditional | flops 4028992 | bytes 8123152 | solution.py:40
  11.8 0.7 pad_maximum_fusion.2
  12.5 1.2 copy.205
  14.1 0.8 bitcast_convert_fusion.3
  17.3 4.5 %conditional.3 = (bf16[16,2,3,3,1,32]{5,2,3,0,4,1:T(4,128)(2,1)}, f32[16,3,1,32,128]{4,3,1,0,2:T(8,128)S(1)}, f32[16,3,1,32,128]{4,3,1,0,2:T(8,128)S(1)}) conditional(s32[]{:T(128)} %bitcast.8, (bf16[16,2,3,1,32,128]{5,4,3,2,1,0:T(8,128)(2,1)S(1)}, bf16[16,2,3,3,1,32]{0,5,3,2,1,4:T(8,128)(2,1)S(1)}) %tuple.150, ...), branch_computations={%region_4.6_spmd.clone.clone, %region_5.7_spmd.clone.clone, %regio... | conditional | flops 4028992 | bytes 8123152 | solution.py:40
  17.3 0.9 copy.218
  18.5 0.7 broadcast_compare_fusion.1
  19.5 0.7 pad_maximum_fusion.9
  20.8 0.6 maximum_select_fusion.4
  21.8 0.8 bitcast_convert_fusion.1
  22.7 0.5 subtract_convert_fusion.4
  24.3 0.5 copy-done.2
  24.9 0.8 convolution_bitcast_fusion.4
  25.6 1.1 fusion.53
  26.7 1.2 fusion.55
  28.2 1.7 pad_maximum_fusion.11
  29.9 2.8 %gather_fusion.1 = f32[32,2,128,128]{2,3,1,0:T(8,128)} fusion(f32[16,2,128,128]{2,3,0,1:T(8,128)S(1)} %pad_maximum_fusion.11, s32[1024]{0:T(1024)S(1)} %pad_clamp_fusion.1), kind=kCustom, calls=%fused_computation.3 | custom fusion | bytes 8388736 | tf_op jit(solution)/shard_map/jit(_take)/gather | solution.py:113
  32.7 4.9 %broadcast_select_fusion = f32[32,2,128,128]{2,3,1,0:T(8,128)} fusion(f32[32,2,128,128]{2,3,1,0:T(8,128)} %gather_fusion.1, pred[32]{0:T(512)(128)(4,1)S(1)} %compare_and_fusion.1), kind=kLoop, calls=%fused_computation.128 | loop fusion | flops 1048576 | bytes 8388640 | tf_op jit(solution)/shard_map/jit(_take)/select_n | solution.py:113
  37.6 0.7 gather_fusion
  38.3 1.6 broadcast_select_fusion.1
  39.9 7.5 %all-to-all-start = ((bf16[32,2,32,512]{3,2,1,0:T(8,128)(2,1)}), bf16[32,2,32,512]{3,2,1,0:T(8,128)(2,1)S(1)}, u32[]{:S(2)}, u32[]{:S(2)}) async-start(bf16[32,2,32,512]{3,2,1,0:T(8,128)(2,1)} %broadcast_select_fusion.1), calls=%async_computation | async-start | bytes 4194304 | tf_op jit(solution)/shard_map/all_to_all | solution.py:118
  47.7 0.6 fusion.74
  49.6 52.6 %all-to-all-done = bf16[32,2,32,512]{3,2,1,0:T(8,128)(2,1)S(1)} async-done(((bf16[32,2,32,512]{3,2,1,0:T(8,128)(2,1)}), bf16[32,2,32,512]{3,2,1,0:T(8,128)(2,1)S(1)}, u32[]{:S(2)}, u32[]{:S(2)}) %all-to-all-start) | async-done | bytes 2097184 | tf_op jit(solution)/shard_map/all_to_all | solution.py:118
  102.6 1.0 copy-done.4
  104.3 1.1 copy.145
  105.5 2.2 %gather_fusion.3 = bf16[8,2,512,128]{3,2,1,0:T(8,128)(2,1)} fusion(bf16[2,512,4,128]{3,1,2,0:T(8,128)(2,1)S(1)} %copy.170, s32[1024]{0:T(1024)S(1)} %pad_clamp_fusion), kind=kCustom, calls=%fused_computation.1.clone | custom fusion | bytes 4194336 | tf_op jit(solution)/shard_map/jit(_take)/gather | solution.py:84
  107.6 2.2 %gather_fusion.2 = bf16[8,2,512,128]{3,2,1,0:T(8,128)(2,1)S(1)} fusion(bf16[2,512,4,128]{3,1,2,0:T(8,128)(2,1)} %copy.145, s32[1024]{0:T(1024)S(1)} %pad_clamp_fusion), kind=kCustom, calls=%fused_computation.clone | custom fusion | bytes 4194336 | tf_op jit(solution)/shard_map/jit(_take)/gather | solution.py:84
  109.8 18.7 %reduce-scatter.2.cloned.1.call-done = f32[2,2,128,128]{2,3,1,0:T(8,128)} async-done(((f32[32,2,128,128]{2,3,1,0:T(8,128)}), f32[2,2,128,128]{2,3,1,0:T(8,128)}) %reduce-scatter.2.cloned.1.call-update) | async-done | bytes 262160 | tf_op jit(solution)/shard_map/reduce_scatter | solution.py:114
  128.5 1.0 convert_element_type.384
  129.5 2.9 %convolution_bitcast_fusion = f32[2,2,2,512,4,128]{3,5,0,4,2,1:T(8,128)S(1)} fusion(bf16[2,4,2,512,128]{4,3,2,1,0:T(8,128)(2,1)} %bitcast.370, pred[2,4]{1,0:T(4,128)(4,1)S(1)} %compare_and_fusion, bf16[2,2,128,128]{2,3,1,0:T(8,128)(2,1)S(1)} %convert_element_type.384), kind=kOutput, calls=%fused_computation.93 | convolution fusion | flops 537919488 | bytes 10551808 | tf_op jit(solution)/shard_map/kab,jdgsb->kjgdsa/dot_general | solution.py:85
  132.4 3.1 %slice_add_fusion.1 = (f32[1,1,2,512,4,128]{3,5,0,4,2,1:T(8,128)}, f32[1,1,2,512,4,128]{3,5,0,4,2,1:T(8,128)}) fusion(f32[2,2,2,512,4,128]{3,5,0,4,2,1:T(8,128)S(1)} %convolution_bitcast_fusion), kind=kLoop, calls=%fused_computation.102 | loop fusion | flops 1048576 | bytes 12582912 | tf_op jit(solution)/shard_map/add | solution.py:89
  135.5 2.9 %copy.189 = f32[1,2,512,512]{3,2,1,0:T(8,128)} copy(f32[1,2,512,512]{2,3,1,0:T(8,128)} %bitcast.375) | data formatting | bytes 4194304 | tf_op jit(solution)/shard_map/sub | solution.py:88
  138.4 3.0 %copy.190 = f32[1,2,512,512]{3,2,1,0:T(8,128)} copy(f32[1,2,512,512]{2,3,1,0:T(8,128)} %bitcast.373) | data formatting | bytes 4194304 | tf_op jit(solution)/shard_map/add | solution.py:89
  141.4 1.3 convolution_bitcast_fusion.1
  142.7 2.3 %slice_add_fusion.2 = (f32[1,1,2,512,4,128]{3,5,0,4,2,1:T(8,128)}, f32[1,1,2,512,4,128]{3,5,0,4,2,1:T(8,128)S(1)}) fusion(f32[2,2,2,512,4,128]{3,5,0,4,2,1:T(8,128)S(1)} %convolution_bitcast_fusion.1), kind=kLoop, calls=%fused_computation.110 | loop fusion | flops 1048576 | bytes 12582912 | tf_op jit(solution)/shard_map/add | solution.py:89
  145.1 1.9 %copy.164 = f32[1,2,512,512]{3,2,1,0:T(8,128)} copy(f32[1,2,512,512]{2,3,1,0:T(8,128)S(1)} %bitcast.376) | data formatting | bytes 4194304 | tf_op jit(solution)/shard_map/sub | solution.py:88
  146.9 3.1 %copy.165 = f32[1,2,512,512]{3,2,1,0:T(8,128)} copy(f32[1,2,512,512]{2,3,1,0:T(8,128)} %bitcast.374) | data formatting | bytes 4194304 | tf_op jit(solution)/shard_map/add | solution.py:89
  150.0 4.2 %subtract_convert_fusion.1 = (bf16[1,2,512,512]{3,2,1,0:T(8,128)(2,1)S(1)}, bf16[1,2,512,512]{3,2,1,0:T(8,128)(2,1)S(1)}, bf16[1,2,512,512]{3,2,1,0:T(8,128)(2,1)S(1)}, bf16[1,2,512,512]{3,2,1,0:T(8,128)(2,1)S(1)}) fusion(f32[1,2,512,512]{3,2,1,0:T(8,128)} %copy.165, f32[1,2,512,512]{3,2,1,0:T(8,128)} %copy.164, f32[2,512]{1,0:T(2,128)S(1)} %bitcast.434, ...), kind=kLoop, calls=%fused_computation.127 | loop fusion | flops 8388608 | bytes 12591104 | tf_op jit(solution)/shard_map/convert.22
  154.3 2.4 %convolution_bitcast_fusion.3 = f32[2,2,2,512,512]{3,4,0,2,1:T(8,128)S(1)} fusion(bf16[2,512,512,1,1]{2,1,0,4,3:T(8,128)(2,1)S(1)} %bitcast.382, bf16[1,2,512,512]{3,2,1,0:T(8,128)(2,1)S(1)} %get-tuple-element.623, bf16[1,2,512,512]{3,2,1,0:T(8,128)(2,1)S(1)} %get-tuple-element.622), kind=kOutput, calls=%fused_computation.96 | convolution fusion | flops 2151677952 | bytes 11534336 | tf_op jit(solution)/shard_map/kcr,jgdr->kjgcd/dot_general | solution.py:97
  157.4 0.9 copy-done.5
  158.3 2.4 %convolution_bitcast_fusion.2 = f32[2,2,2,512,512]{3,4,2,1,0:T(8,128)S(1)} fusion(bf16[2,512,512,1,1]{2,1,4,3,0:T(8,128)(2,1)S(1)} %bitcast.381, bf16[1,2,512,512]{3,2,1,0:T(8,128)(2,1)S(1)} %get-tuple-element.682, bf16[1,2,512,512]{3,2,1,0:T(8,128)(2,1)S(1)} %get-tuple-element.683), kind=kOutput, calls=%fused_computation.95 | convolution fusion | flops 2151677952 | bytes 11534336 | tf_op jit(solution)/shard_map/kcr,jgdr->kjgcd/dot_general | solution.py:97
  160.7 0.8 fusion.41
  162.3 2.4 %pad_maximum_fusion.10 = bf16[2,2,2,512,512]{3,4,1,2,0:T(8,128)(2,1)} fusion(bf16[1,2,2,512,512]{3,4,1,2,0:T(8,128)(2,1)S(1)} %fusion.39, bf16[1,2,2,512,512]{3,4,1,2,0:T(8,128)(2,1)S(1)} %fusion.38), kind=kLoop, calls=%fused_computation.92 | loop fusion | flops 2097152 | bytes 8388608 | tf_op jit(solution)/shard_map/stack | solution.py:126
  164.7 7.3 %copy.176 = bf16[2,2,2,512,512]{4,3,2,1,0:T(8,128)(2,1)} copy(bf16[2,2,2,512,512]{3,4,1,2,0:T(8,128)(2,1)} %pad_maximum_fusion.10) | data formatting | bytes 8388608 | tf_op jit(solution)/shard_map/stack | solution.py:126
  (77 shorter events, 8.6 us)
Async XLA Ops:
  6.5 31.1 %copy-start = (bf16[16,2,32,512]{3,2,1,0:T(8,128)(2,1)S(1)}, bf16[16,2,32,512]{3,2,1,0:T(8,128)(2,1)}, u32[]{:S(2)}) copy-start(bf16[16,2,32,512]{3,2,1,0:T(8,128)(2,1)} %param.22) | copy-start | bytes 3145732
  6.5 122.0 %reduce-scatter.2.cloned.1.call-start = ((), (), s32[]{:S(2)}) async-start(), calls=%async_computation.2 | async-start | bytes 4456448 | tf_op jit(solution)/shard_map/reduce_scatter | solution.py:114
  19.2 1.5 copy-start.16
  23.7 1.1 copy-start.2
  26.7 1.2 copy-start.10
  39.9 7.5 %copy-start.12 = (s32[2,4]{1,0:T(2,128)S(1)}, s32[2,4]{1,0:T(2,128)}, u32[]{:S(2)}) copy-start(s32[2,4]{1,0:T(2,128)} %param.20) | copy-start | bytes 100
  39.9 7.6 %copy-start.11 = (s32[2,4]{1,0:T(2,128)S(1)}, s32[2,4]{1,0:T(2,128)}, u32[]{:S(2)}) copy-start(s32[2,4]{1,0:T(2,128)} %param.21) | copy-start | bytes 100
  39.9 62.2 %all-to-all-start = ((bf16[32,2,32,512]{3,2,1,0:T(8,128)(2,1)}), bf16[32,2,32,512]{3,2,1,0:T(8,128)(2,1)S(1)}, u32[]{:S(2)}, u32[]{:S(2)}) async-start(bf16[32,2,32,512]{3,2,1,0:T(8,128)(2,1)} %broadcast_select_fusion.1), calls=%async_computation | async-start | bytes 4194304 | tf_op jit(solution)/shard_map/all_to_all | solution.py:118
  102.6 1.0 copy-start.4
  102.6 1.4 copy-start.6
  146.9 3.1 %copy-start.3 = (f32[1,2,512,512]{3,2,1,0:T(8,128)S(1)}, f32[1,2,512,512]{3,2,1,0:T(8,128)}, u32[]{:S(2)}) copy-start(f32[1,2,512,512]{3,2,1,0:T(8,128)} %copy.189) | copy-start | bytes 6291460
  150.0 4.2 %copy-start.7 = (bf16[1,2,16,32,512]{4,3,2,1,0:T(8,128)(2,1)S(1)}, bf16[1,2,16,32,512]{4,3,2,1,0:T(8,128)(2,1)}, u32[]{:S(2)}) copy-start(bf16[1,2,16,32,512]{4,3,2,1,0:T(8,128)(2,1)} %copy-done.6) | copy-start | bytes 3145732
  157.1 1.2 copy-start.5
  164.7 7.4 %copy-start.1 = (bf16[16,2,32,512]{3,2,1,0:T(8,128)(2,1)S(1)}, bf16[16,2,32,512]{3,2,1,0:T(8,128)(2,1)}, u32[]{:S(2)}) copy-start(bf16[16,2,32,512]{3,2,1,0:T(8,128)(2,1)} %param.22) | copy-start | bytes 3145732
Sparse Core Ops, SparseCore 0:
  37.7 90.7 reduce-scatter.1
where the time goes:
time: 180 us; the launch traced here: 179 us
  waiting for transfers between devices  71.3 us (40%)
  local copies, waits for them, and re-layouts  38.2 us (21%)
  other arithmetic  35.4 us (20%)
  between operations  16.3 us (9%)
  matrix products  9.74 us (5%)
  starting transfers between devices  7.52 us (4%)
    all_to_all x1, waiting for transfers between devices, shards(): lax.all_to_all(outgoing, 'src', split_axis=0, concat_axis=2, tiled=True)  52.6 us
    reduce_scatter x1, waiting for transfers between devices, shards(): lax.psum_scatter(outbound, 'src', scatter_dimension=0, tiled=True)  18.7 us
    all_to_all x1, starting transfers between devices, shards(): lax.all_to_all(outgoing, 'src', split_axis=0, concat_axis=2, tiled=True)  7.52 us
    another operation x1, local copies, waits for them, and re-layouts, shards(): return jnp.stack(results, 0)  7.35 us
    another operation x7, other arithmetic  7.13 us
    add x2, local copies, waits for them, and re-layouts, triple(): imag_part = products[0, 1] + products[1, 0]  6.07 us
    add x2, other arithmetic, triple(): imag_part = products[0, 1] + products[1, 0]  5.41 us
    select_n x1, other arithmetic, shards(): outbound = jnp.take(partial_value, listed, axis=0)  4.91 us
  transfers between devices with their start and end apart: 2, of which 2 were waited for; matrix products, arithmetic and copies ran while one was open for 5% of the time, Pallas kernels for 0%

commit v1 on v0

v1 whole, which is shorter than its diff:
```python
import functools

import jax
import jax.numpy as jnp
from jax import lax
from jax.experimental import pallas as pl
from jax.experimental.pallas import tpu as pltpu
from jax.sharding import PartitionSpec as P

F32 = jnp.float32
BF16 = jnp.bfloat16
QUAD = 4


def hop_tables(gauge_links, hop_path):
    time_count, side_y, side_z = gauge_links.shape[0], gauge_links.shape[6], gauge_links.shape[7]
    sites = side_y * side_z
    links = gauge_links.reshape(time_count, 2, 2, 3, 3, sites)
    site = jnp.arange(sites)
    ypos, zpos = site // side_z, site % side_z
    up_y = ((ypos + 1) % side_y) * side_z + zpos
    up_z = ypos * side_z + (zpos + 1) % side_z
    step_up = jnp.where((hop_path < 2)[:, None], up_y[None], up_z[None])
    minus = (hop_path % 2) == 1
    up = (step_up[:, :, None] == site[None, None, :]).astype(BF16)
    mask = jnp.where(minus[:, None, None], jnp.swapaxes(up, 1, 2), up)
    axis = jnp.where((hop_path < 2)[None, :, None, None, None, None], links[:, None, 0], links[:, None, 1])
    mover = jnp.where(minus[:, None, None], jnp.eye(sites, dtype=BF16)[None], up)
    moved = jnp.einsum("thkcdx,hxy->thkcdy", axis, mover, preferred_element_type=F32)
    flipped = jnp.swapaxes(moved, 3, 4) * jnp.array([1.0, -1.0], F32)[None, None, :, None, None, None]
    rows = jnp.where(minus[None, :, None, None, None, None], flipped, moved)
    rows = rows.reshape(time_count, hop_path.shape[0], 6, 3 * sites)
    return rows, jnp.tile(mask.astype(F32), (1, 1, 3))


def exchange_kernel(
    n, hops, times_ref, pera_ref, eig_ref, rows_ref, mask_ref,
    blocks_ref, elem_ref,
    pstage, epart, estage, erecv, fstage, frecv,
    psend, precv, plocal, qsend, qrecv, zsend, zrecv,
):
    me = lax.axis_index("src")
    slots = blocks_ref.shape[0]
    time_count = eig_ref.shape[0]
    rings = n // QUAD
    mine_q, mine_z = lax.rem(me, QUAD), me // QUAD

    barrier = pltpu.get_barrier_semaphore()

    @pl.loop(1, n)
    def _(o):
        pl.semaphore_signal(barrier, inc=1, device_id={"src": lax.rem(me + o, n)})

    @pl.loop(0, n)
    def _(d):
        for s in range(slots):
            pstage[d, s] = pera_ref[times_ref[d * slots + s]]

    pl.semaphore_wait(barrier, n - 1)

    def pera_copy(o, s, origin):
        peer = lax.rem(me + o, n)
        return pltpu.make_async_remote_copy(
            src_ref=pstage.at[peer, s], dst_ref=blocks_ref.at[s, origin],
            send_sem=psend.at[s, o], recv_sem=precv.at[s, o], device_id={"src": peer},
        )

    for s in range(slots):
        pltpu.make_async_copy(pstage.at[me, s], blocks_ref.at[s, me], plocal.at[s]).start()

    def send_slot(s):
        @pl.loop(1, n)
        def _(o):
            pera_copy(o, s, me).start()

    send_slot(0)

    def one_time(t, carry):
        vec = eig_ref[t]
        cur = vec
        half = vec.shape[0] // 2
        for h in range(hops):
            mask = mask_ref[h]
            row = rows_ref[t, h]
            re = jnp.concatenate([mask * row[c : c + 1] for c in range(3)], 0)
            im = jnp.concatenate([mask * row[3 + c : 4 + c] for c in range(3)], 0)
            re, im, neg = re.astype(BF16), im.astype(BF16), (-im).astype(BF16)
            top, low = cur[:half], cur[half:]
            out_re = jnp.dot(re, top, preferred_element_type=F32) + jnp.dot(neg, low, preferred_element_type=F32)
            out_im = jnp.dot(im, top, preferred_element_type=F32) + jnp.dot(re, low, preferred_element_type=F32)
            cur = jnp.concatenate([out_re, out_im], 0).astype(BF16)
        turned = jnp.concatenate([cur[half:], -cur[:half]], 0)
        both = jnp.concatenate([cur, turned], 1)
        part = lax.dot_general(vec, both, (((0,), (0,)), ((), ())), preferred_element_type=F32)
        epart[t] = part.astype(BF16)
        return carry

    lax.fori_loop(0, time_count, one_time, 0, unroll=4)

    @pl.loop(0, rings)
    def _(z):
        for q in range(QUAD):
            for s in range(slots):
                estage[q, z * slots + s] = epart[times_ref[(z * QUAD + q) * slots + s]]

    def quad_copy(o, origin):
        peer = lax.rem(mine_q + o, QUAD)
        return pltpu.make_async_remote_copy(
            src_ref=estage.at[peer], dst_ref=erecv.at[origin],
            send_sem=qsend.at[o], recv_sem=qrecv.at[o], device_id={"src": mine_z * QUAD + peer},
        )

    for o in range(1, QUAD):
        quad_copy(o, mine_q).start()
    for s in range(1, slots):
        send_slot(s)
    for o in range(1, QUAD):
        quad_copy(o, lax.rem(mine_q + QUAD - o, QUAD)).wait()

    @pl.loop(0, rings * slots)
    def _(j):
        total = estage[mine_q, j].astype(F32)
        for o in range(1, QUAD):
            total += erecv[lax.rem(mine_q + o, QUAD), j].astype(F32)
        fstage[j // slots, lax.rem(j, slots)] = total.astype(BF16)

    def ring_copy(o, origin):
        peer = lax.rem(mine_z + o, rings)
        return pltpu.make_async_remote_copy(
            src_ref=fstage.at[peer], dst_ref=frecv.at[origin],
            send_sem=zsend.at[o], recv_sem=zrecv.at[o], device_id={"src": peer * QUAD + mine_q},
        )

    for o in range(1, rings):
        ring_copy(o, mine_z).start()
    for o in range(1, rings):
        ring_copy(o, lax.rem(mine_z + rings - o, rings)).wait()
    total = fstage[mine_z].astype(F32)
    for o in range(1, rings):
        total += frecv[lax.rem(mine_z + o, rings)].astype(F32)
    elem_ref[...] = total.astype(BF16)

    for s in range(slots):
        pltpu.make_async_copy(pstage.at[me, s], blocks_ref.at[s, me], plocal.at[s]).wait()

        @pl.loop(1, n)
        def _(o):
            pera_copy(o, s, lax.rem(me + n - o, n)).wait()


def triple_kernel(perm_ref, phase_ref, mine_ref, blocks_ref, elem_ref, out_ref, left, turned):
    slot, group = pl.program_id(0), pl.program_id(1)
    order = out_ref.shape[-1]
    width = elem_ref.shape[1]
    spins = order // width

    @pl.when(group == 0)
    def _():
        elem = elem_ref[0]
        re = blocks_ref[0, :, 0].reshape(order, order)
        im = blocks_ref[0, :, 1].reshape(order, order)
        left[:, :order] = re
        left[:, order:] = im
        for spin in range(spins):
            part_re = re[:, spin * width : (spin + 1) * width]
            part_im = im[:, spin * width : (spin + 1) * width]
            dims = (((1,), (1,)), ((), ()))
            turned[spin, 0] = lax.dot_general(
                elem, jnp.concatenate([part_re, -part_im], 1), dims, preferred_element_type=F32
            ).astype(BF16)
            turned[spin, 1] = lax.dot_general(
                elem, jnp.concatenate([part_im, part_re], 1), dims, preferred_element_type=F32
            ).astype(BF16)

    reals, imags = [], []
    for spin in range(spins):
        source = perm_ref[group, spin]
        phase = phase_ref[group, spin]
        scale_re = (phase == 0).astype(F32) - (phase == 2).astype(F32)
        scale_im = (phase == 1).astype(F32) - (phase == 3).astype(F32)
        re = turned[source, 0].astype(F32)
        im = turned[source, 1].astype(F32)
        reals.append((scale_re * re - scale_im * im).astype(BF16))
        imags.append((scale_re * im + scale_im * re).astype(BF16))
    real, imag = jnp.concatenate(reals, 0), jnp.concatenate(imags, 0)
    filled = mine_ref[slot] >= 0
    lhs = left[...]
    for part, right in enumerate((jnp.concatenate([real, imag], 0), jnp.concatenate([imag, -real], 0))):
        result = jnp.dot(lhs, right, preferred_element_type=F32)
        out_ref[0, 0, part] = jnp.where(filled, result, 0.0).astype(BF16)


def shards(n, eigenvectors, gauge_links, hop_path, spin_perm, spin_phase, perambulators, owned_times):
    time_count = eigenvectors.shape[0]
    width = eigenvectors.shape[-1]
    slots = owned_times.shape[1]
    rows, order = perambulators.shape[2], perambulators.shape[3]
    groups = spin_perm.shape[0]
    hops = hop_path.shape[0]
    rings = n // QUAD
    listed = jnp.clip(owned_times.reshape(-1), 0, time_count - 1)
    mine = lax.dynamic_index_in_dim(owned_times, lax.axis_index("src"), 0, keepdims=False)
    eig = eigenvectors.reshape(time_count, -1, width)
    link_rows, mask = hop_tables(gauge_links, hop_path)
    vmem = pl.BlockSpec(memory_space=pltpu.VMEM)
    smem = pl.BlockSpec(memory_space=pltpu.SMEM)
    blocks, elem = pl.pallas_call(
        functools.partial(exchange_kernel, n, hops),
        out_shape=(
            jax.ShapeDtypeStruct((slots, n, 2, rows, order), BF16),
            jax.ShapeDtypeStruct((slots, width, 2 * width), BF16),
        ),
        in_specs=[smem, vmem, vmem, vmem, vmem],
        out_specs=(pl.BlockSpec(memory_space=pl.ANY), vmem),
        scratch_shapes=[
            pltpu.VMEM((n, slots, 2, rows, order), BF16),
            pltpu.VMEM((time_count, width, 2 * width), BF16),
            pltpu.VMEM((QUAD, rings * slots, width, 2 * width), BF16),
            pltpu.VMEM((QUAD, rings * slots, width, 2 * width), BF16),
            pltpu.VMEM((rings, slots, width, 2 * width), BF16),
            pltpu.VMEM((rings, slots, width, 2 * width), BF16),
            pltpu.SemaphoreType.DMA((slots, n)),
            pltpu.SemaphoreType.DMA((slots, n)),
            pltpu.SemaphoreType.DMA((slots,)),
            pltpu.SemaphoreType.DMA((QUAD,)),
            pltpu.SemaphoreType.DMA((QUAD,)),
            pltpu.SemaphoreType.DMA((rings,)),
            pltpu.SemaphoreType.DMA((rings,)),
        ],
        compiler_params=pltpu.CompilerParams(
            collective_id=0, has_side_effects=True, vmem_limit_bytes=48 * 2**20
        ),
        name="exchange",
    )(listed, perambulators, eig, link_rows, mask)
    return pl.pallas_call(
        triple_kernel,
        grid=(slots, groups),
        out_shape=jax.ShapeDtypeStruct((slots, groups, 2, order, order), BF16),
        in_specs=[
            smem,
            smem,
            smem,
            pl.BlockSpec((1, n, 2, rows, order), lambda s, g: (s, 0, 0, 0, 0)),
            pl.BlockSpec((1, width, 2 * width), lambda s, g: (s, 0, 0)),
        ],
        out_specs=pl.BlockSpec((1, 1, 2, order, order), lambda s, g: (s, g, 0, 0, 0)),
        scratch_shapes=[
            pltpu.VMEM((order, 2 * order), BF16),
            pltpu.VMEM((order // width, 2, width, order), BF16),
        ],
        compiler_params=pltpu.CompilerParams(
            dimension_semantics=("arbitrary", "arbitrary"), vmem_limit_bytes=40 * 2**20
        ),
        name="triple",
    )(spin_perm, spin_phase, mine, blocks, elem)


def solution(mesh):
    in_specs = (
        P("groups", None, None, "src", None, None, None),
        P("groups", None, None, None, None, "src", None, None),
        P("groups"),
        P("groups", None),
        P("groups", None),
        P("groups", None, "src", None),
        P("groups", None),
    )
    out_specs = P(("groups", "src"), None, None, None, None)
    return jax.shard_map(
        functools.partial(shards, mesh.shape["src"]),
        mesh=mesh, in_specs=in_specs, out_specs=out_specs, check_vma=False,
    )
```

time: 180 us -> 78.1 us (0.43)
  Pallas kernels: 0 us -> 72 us
  waiting for transfers between devices: 71.3 us -> 0 us
  local copies, waits for them, and re-layouts: 38.2 us -> 2.91 us
  other arithmetic: 35.4 us -> 2.27 us
  between operations: 16.3 us -> 0.09 us
  matrix products: 9.74 us -> 0.25 us
  starting transfers between devices: 7.52 us -> 0 us
    pallas_call x0 -> x2, Pallas kernels: none -> 72 us  [the longest x1 63.3 us: shards(): pl.pallas_call(functools.partial(exchange_kernel, n, hops), out_shape=(ja...]
    all_to_all x1 -> x0, waiting for transfers between devices: 52.6 us -> none  [shards(): lax.all_to_all(outgoing, 'src', split_axis=0, concat_axis=2, tiled=True)]
    reduce_scatter x1 -> x0, waiting for transfers between devices: 18.7 us -> none  [shards(): lax.psum_scatter(outbound, 'src', scatter_dimension=0, tiled=True)]
    another operation x21 -> x0, other arithmetic: 14.6 us -> none
    another operation x9 -> x2, local copies, waits for them, and re-layouts: 11.5 us -> 0.13 us  [hop_tables(): return (rows, jnp.tile(mask.astype(F32), (1, 1, 3)))]
    dot_general x5 -> x1, matrix products: 9.74 us -> 0.25 us  [hop_tables(): jnp.einsum('thkcdx,hxy->thkcdy', axis, mover, preferred_element_type=F32)]
    gather x4 -> x0, local copies, waits for them, and re-layouts: 7.85 us -> none  [the longest x2 4.34 us: triple(): permuted = jnp.take(columns, spin_perm, axis=2)]
    select_n x8 -> x2, other arithmetic: 8.48 us -> 0.83 us  [the longest x1 0.75 us: hop_tables(): rows = jnp.where(minus[None, :, None, None, None, None], flipped, moved)]
  transfers between devices with their start and end apart: 2 -> 0, of which waited for: 2 -> 0; matrix products, arithmetic and copies ran while one was open for 5% -> 0% of each run, Pallas kernels for 0% -> 0%
where the time goes in v1:
time: 78.1 us; the launch traced here: 77.5 us
  Pallas kernels  72 us (92%)
  local copies, waits for them, and re-layouts  2.91 us (4%)
  other arithmetic  2.27 us (3%)
    pallas_call x1, Pallas kernels, shards(): pl.pallas_call(functools.partial(exchange_kernel, n, hops), out_shape=(ja...  63.3 us
    pallas_call x1, Pallas kernels, shards(): pl.pallas_call(triple_kernel, grid=(slots, groups), out_shape=jax.ShapeDt...  8.71 us

profile of v1, /device:TPU:0, one launch (start us, length us, event | category | flops | bytes accessed | tf_op | source)
XLA Modules:
  0.0 77.5 jit_solution(18254618906408777762)
XLA Ops:
  0.0 0.0 copy-start
  0.0 0.0 copy-start.3
  0.0 0.0 copy-start.2
  0.0 0.0 copy-start.1
  0.0 1.0 %dynamic-slice_reduce_fusion.mine_ref = s32[2]{0:T(128)S(1)} fusion(s32[16,2]{0,1:T(2,128)} %param.14, s32[]{:T(128)S(6)} %select_n.84), kind=kLoop, calls=%fused_computation.36 | loop fusion | bytes 20 | tf_op jit(solution)/shard_map/jit(dynamic_index_in_dim)/dynamic_slice | solution.py:202
  1.0 0.7 broadcast_clamp_fusion
  1.7 0.7 fusion.17
  2.4 0.1 broadcast_select_fusion
  2.4 0.1 copy.14
  2.5 0.1 min.12.times_ref
  2.6 0.1 fusion.11
  2.7 0.1 tile.10.mask_ref
  2.8 1.0 %slice_bitcast_fusion.1 = (bf16[16,2,3,3,32]{0,4,3,2,1:T(8,128)(2,1)S(1)}, bf16[16,2,3,3,32]{0,4,3,2,1:T(8,128)(2,1)S(1)}) fusion(bf16[16,2,2,3,3,32]{0,5,4,3,2,1:T(8,128)(2,1)} %bitcast.16), kind=kLoop, calls=%fused_computation.3 | loop fusion | bytes 73728 | tf_op jit(solution)/shard_map/jit(_where)/broadcast_in_dim | solution.py:27
  3.9 0.1 copy.15
  4.0 0.1 copy.16
  4.1 0.2 fusion
  4.4 0.8 bitcast_select_fusion
  5.1 0.2 copy.21
  5.3 0.2 reshape.132.rows_ref
  5.5 0.0 copy-done
  5.5 0.0 copy-done.1
  5.5 63.3 %exchange.1 = (bf16[2,16,2,32,512]{4,3,2,1,0:T(8,128)(2,1)S(1)}, bf16[2,128,256]{2,1,0:T(8,128)(2,1)S(1)}) custom-call(s32[32]{0:T(128)S(1)} %min.12.times_ref, bf16[16,2,32,512]{3,2,1,0:T(8,128)(2,1)S(1)} %copy-done, bf16[16,192,128]{2,1,0:T(8,128)(2,1)S(1)} %bitcast.15, f32[16,2,6,96]{3,2,1,0:T(8,128)S(1)} %reshape.132.rows_ref, ...), custom_call_target="tpu_custom_call" | custom-call | tf_op jit(solution)/shard_map/exchange/pallas_call | solution.py:207
  68.7 0.0 copy-done.3
  68.8 0.0 copy-done.2
  68.8 8.7 %triple.1 = bf16[2,2,2,512,512]{4,3,2,1,0:T(8,128)(2,1)} custom-call(s32[2,4]{1,0:T(2,128)S(1)} %copy-done.2, s32[2,4]{1,0:T(2,128)S(1)} %copy-done.3, s32[2]{0:T(128)S(1)} %dynamic-slice_reduce_fusion.mine_ref, bf16[2,16,2,32,512]{4,3,2,1,0:T(8,128)(2,1)S(1)} %get-tuple-element.7.blocks_ref, bf16[2,128,256]{2,1,0:T(8,128)(2,1)S(1)} %get-tuple-element.8.elem_ref), custom_call_target="tpu_custom_call" | custom-call | tf_op jit(solution)/shard_map/triple/pallas_call | solution.py:235
  (3 shorter events, 0.0 us)
Async XLA Ops:
  0.0 5.5 %copy-start = (bf16[16,2,32,512]{3,2,1,0:T(8,128)(2,1)S(1)}, bf16[16,2,32,512]{3,2,1,0:T(8,128)(2,1)}, u32[]{:S(2)}) copy-start(bf16[16,2,32,512]{3,2,1,0:T(8,128)(2,1)} %pera_ref.1) | copy-start | bytes 3145732
  0.0 68.7 %copy-start.3 = (s32[2,4]{1,0:T(2,128)S(1)}, s32[2,4]{1,0:T(2,128)}, u32[]{:S(2)}) copy-start(s32[2,4]{1,0:T(2,128)} %phase_ref.1) | copy-start | bytes 100
  0.0 68.8 %copy-start.2 = (s32[2,4]{1,0:T(2,128)S(1)}, s32[2,4]{1,0:T(2,128)}, u32[]{:S(2)}) copy-start(s32[2,4]{1,0:T(2,128)} %perm_ref.1) | copy-start | bytes 100
  0.0 5.5 %copy-start.1 = (bf16[16,2,3,1,8,4,128]{6,5,4,3,2,1,0:T(4,128)(2,1)S(1)}, bf16[16,2,3,1,8,4,128]{6,5,4,3,2,1,0:T(4,128)(2,1)}, u32[]{:S(2)}) copy-start(bf16[16,2,3,1,8,4,128]{6,5,4,3,2,1,0:T(4,128)(2,1)} %param.8) | copy-start | bytes 2359300

commit v2 on v1

v2 whole, which is shorter than its diff:
```python
import functools

import jax
import jax.numpy as jnp
import numpy as np
from jax import lax
from jax.experimental import pallas as pl
from jax.experimental.pallas import tpu as pltpu
from jax.sharding import PartitionSpec as P

F32 = jnp.float32
BF16 = jnp.bfloat16
QUAD = 4


def site_tables(side_y, side_z):
    sites = side_y * side_z
    site = np.arange(sites)
    ypos, zpos = site // side_z, site % side_z
    up_y = ((ypos + 1) % side_y) * side_z + zpos
    up_z = ypos * side_z + (zpos + 1) % side_z
    masks, movers = [], []
    for target in (up_y, up_z):
        up = (target[:, None] == site[None, :]).astype(np.float32)
        masks += [up, up.T]
        movers += [up, np.eye(sites, dtype=np.float32)]
    masks = np.stack([np.tile(m, (1, 3)) for m in masks])
    movers = np.stack([np.kron(np.eye(3, dtype=np.float32), m) for m in movers])
    return masks, movers


def exchange_kernel(
    n, hops, owned_ref, hop_ref, pera_ref, eig_ref, links_ref, masks_ref, movers_ref,
    blocks_ref, elem_ref,
    pstage, epart, rows_ref, hopmask, sends, recvs, keeps,
    psend, precv, plocal, esend, erecv,
):
    me = lax.axis_index("src")
    slots = blocks_ref.shape[0]
    time_count = eig_ref.shape[0]
    rings = n // QUAD
    stages = n.bit_length() - 1
    mine_q, mine_z = lax.rem(me, QUAD), me // QUAD

    def listed(d, s):
        return jnp.minimum(jnp.maximum(owned_ref[d, s], 0), time_count - 1)

    barrier = pltpu.get_barrier_semaphore()

    @pl.loop(1, n)
    def _(o):
        pl.semaphore_signal(barrier, inc=1, device_id={"src": lax.rem(me + o, n)})

    @pl.loop(0, n)
    def _(d):
        for s in range(slots):
            pstage[d, s] = pera_ref[listed(d, s)]

    pl.semaphore_wait(barrier, n - 1)

    def pera_copy(dz, dq, s, receive):
        peer = lax.rem(mine_z + dz, rings) * QUAD + lax.rem(mine_q + dq, QUAD)
        source = lax.rem(mine_z + rings - dz, rings) * QUAD + lax.rem(mine_q + QUAD - dq, QUAD)
        return pltpu.make_async_remote_copy(
            src_ref=pstage.at[peer, s], dst_ref=blocks_ref.at[s, source if receive else me],
            send_sem=psend.at[s, dz, dq], recv_sem=precv.at[s, dz, dq], device_id={"src": peer},
        )

    def local_copy(s):
        return pltpu.make_async_copy(pstage.at[me, s], blocks_ref.at[s, me], plocal.at[s])

    def send_far(s):
        @pl.loop(0, rings - 1)
        def _(i):
            dz = lax.rem(i + rings // 2 - 1, rings - 1) + 1
            for dq in range(QUAD):
                pera_copy(dz, dq, s, False).start()

    def send_near(s):
        local_copy(s).start()
        for dq in range(1, QUAD):
            pera_copy(0, dq, s, False).start()

    def wait_slot(s):
        @pl.loop(0, rings - 1)
        def _(i):
            for dq in range(QUAD):
                pera_copy(i + 1, dq, s, True).wait()

        for dq in range(1, QUAD):
            pera_copy(0, dq, s, True).wait()
        local_copy(s).wait()

    send_far(0)

    for h in range(hops):
        code = hop_ref[h]
        pick = [(code == i).astype(F32) for i in range(4)]
        hopmask[h] = sum(pick[i] * masks_ref[i] for i in range(4))
        mover = sum(pick[i] * movers_ref[i] for i in range(4)).astype(BF16)
        for k in range(2):
            sign = 1.0 - 2.0 * k
            for c in range(3):
                stack = []
                for d in range(3):
                    here, flip = k * 9 + c * 3 + d, k * 9 + d * 3 + c
                    stack.append(
                        pick[0] * links_ref[here].astype(F32)
                        + (sign * pick[1]) * links_ref[flip].astype(F32)
                        + pick[2] * links_ref[18 + here].astype(F32)
                        + (sign * pick[3]) * links_ref[18 + flip].astype(F32)
                    )
                rows_ref[h, k * 3 + c] = lax.dot_general(
                    jnp.concatenate(stack, 0).astype(BF16), mover, (((0,), (0,)), ((), ())),
                    preferred_element_type=F32,
                )

    def one_time(t, carry):
        vec = eig_ref[t]
        cur = vec
        half = vec.shape[0] // 2
        for h in range(hops):
            mask = hopmask[h]
            row = [rows_ref[h, i, pl.ds(t, 1), :] for i in range(6)]
            re = jnp.concatenate([mask * row[c] for c in range(3)], 0)
            im = jnp.concatenate([mask * row[3 + c] for c in range(3)], 0)
            re, im, neg = re.astype(BF16), im.astype(BF16), (-im).astype(BF16)
            top, low = cur[:half], cur[half:]
            out_re = jnp.dot(re, top, preferred_element_type=F32) + jnp.dot(neg, low, preferred_element_type=F32)
            out_im = jnp.dot(im, top, preferred_element_type=F32) + jnp.dot(re, low, preferred_element_type=F32)
            cur = jnp.concatenate([out_re, out_im], 0).astype(BF16)
        turned = jnp.concatenate([cur[half:], -cur[:half]], 0)
        both = jnp.concatenate([cur, turned], 1)
        epart[t] = lax.dot_general(vec, both, (((0,), (0,)), ((), ())), preferred_element_type=F32)
        return carry

    lax.fori_loop(0, time_count, one_time, 0, unroll=4)

    for s in range(1, slots):
        send_far(s)

    def elem_copy(b):
        bit = lax.rem(me // (1 << b), 2)
        return pltpu.make_async_remote_copy(
            src_ref=sends[b], dst_ref=recvs[b], send_sem=esend.at[b], recv_sem=erecv.at[b],
            device_id={"src": me + (1 << b) * (1 - 2 * bit)},
        )

    for b in range(stages):
        bit = lax.rem(me // (1 << b), 2)
        count = n >> (b + 1)

        def value(i, s, b=b):
            if b == 0:
                return epart[listed(i, s)]
            return keeps[b - 1][i, s] + recvs[b - 1][i, s].astype(F32)

        @pl.loop(0, count)
        def _(i):
            for s in range(slots):
                sends[b][i, s] = value(2 * i + 1 - bit, s).astype(sends[b].dtype)

        elem_copy(b).start()

        @pl.loop(0, count)
        def _(i):
            for s in range(slots):
                keeps[b][i, s] = value(2 * i + bit, s)

        elem_copy(b).wait()
    elem_ref[...] = (keeps[stages - 1][0] + recvs[stages - 1][0].astype(F32)).astype(BF16)

    for s in range(slots):
        send_near(s)
    for s in range(slots):
        wait_slot(s)


def triple_kernel(perm_ref, phase_ref, owned_ref, blocks_ref, elem_ref, out_ref, left, turned):
    slot, group = pl.program_id(0), pl.program_id(1)
    order = out_ref.shape[-1]
    width = elem_ref.shape[1]
    spins = order // width

    @pl.when(group == 0)
    def _():
        elem = elem_ref[0]
        re = blocks_ref[0, :, 0].reshape(order, order)
        im = blocks_ref[0, :, 1].reshape(order, order)
        left[:, :order] = re
        left[:, order:] = im
        for spin in range(spins):
            part_re = re[:, spin * width : (spin + 1) * width]
            part_im = im[:, spin * width : (spin + 1) * width]
            dims = (((1,), (1,)), ((), ()))
            turned[spin, 0] = lax.dot_general(
                elem, jnp.concatenate([part_re, -part_im], 1), dims, preferred_element_type=F32
            ).astype(BF16)
            turned[spin, 1] = lax.dot_general(
                elem, jnp.concatenate([part_im, part_re], 1), dims, preferred_element_type=F32
            ).astype(BF16)

    reals, imags = [], []
    for spin in range(spins):
        source = perm_ref[group, spin]
        phase = phase_ref[group, spin]
        scale_re = (phase == 0).astype(F32) - (phase == 2).astype(F32)
        scale_im = (phase == 1).astype(F32) - (phase == 3).astype(F32)
        re = turned[source, 0].astype(F32)
        im = turned[source, 1].astype(F32)
        reals.append((scale_re * re - scale_im * im).astype(BF16))
        imags.append((scale_re * im + scale_im * re).astype(BF16))
    real, imag = jnp.concatenate(reals, 0), jnp.concatenate(imags, 0)
    filled = owned_ref[lax.axis_index("src"), slot] >= 0
    lhs = left[...]
    for part, right in enumerate((jnp.concatenate([real, imag], 0), jnp.concatenate([imag, -real], 0))):
        result = jnp.dot(lhs, right, preferred_element_type=F32)
        out_ref[0, 0, part] = jnp.where(filled, result, 0.0).astype(BF16)


def shards(n, eigenvectors, gauge_links, hop_path, spin_perm, spin_phase, perambulators, owned_times):
    time_count = eigenvectors.shape[0]
    width = eigenvectors.shape[-1]
    slots = owned_times.shape[1]
    rows, order = perambulators.shape[2], perambulators.shape[3]
    groups = spin_perm.shape[0]
    hops = hop_path.shape[0]
    rings = n // QUAD
    side_y, side_z = eigenvectors.shape[4], eigenvectors.shape[5]
    sites = side_y * side_z
    eig = eigenvectors.reshape(time_count, -1, width)
    links = jnp.transpose(gauge_links.reshape(time_count, 36, sites), (1, 2, 0))
    masks, movers = site_tables(side_y, side_z)
    stages = n.bit_length() - 1
    tile = (slots, width, 2 * width)
    vmem = pl.BlockSpec(memory_space=pltpu.VMEM)
    smem = pl.BlockSpec(memory_space=pltpu.SMEM)
    parts = [pltpu.VMEM((n >> (b + 1),) + tile, F32 if b == 0 else BF16) for b in range(stages)]
    blocks, elem = pl.pallas_call(
        functools.partial(exchange_kernel, n, hops),
        out_shape=(
            jax.ShapeDtypeStruct((slots, n, 2, rows, order), BF16),
            jax.ShapeDtypeStruct(tile, BF16),
        ),
        in_specs=[smem, smem] + [vmem] * 5,
        out_specs=(pl.BlockSpec(memory_space=pl.ANY), vmem),
        scratch_shapes=[
            pltpu.VMEM((n, slots, 2, rows, order), BF16),
            pltpu.VMEM((time_count, width, 2 * width), F32),
            pltpu.VMEM((hops, 6, time_count, 3 * sites), F32),
            pltpu.VMEM((hops, sites, 3 * sites), F32),
            parts,
            parts,
            [pltpu.VMEM((n >> (b + 1),) + tile, F32) for b in range(stages)],
            pltpu.SemaphoreType.DMA((slots, rings, QUAD)),
            pltpu.SemaphoreType.DMA((slots, rings, QUAD)),
            pltpu.SemaphoreType.DMA((slots,)),
            pltpu.SemaphoreType.DMA((stages,)),
            pltpu.SemaphoreType.DMA((stages,)),
        ],
        compiler_params=pltpu.CompilerParams(
            collective_id=0, has_side_effects=True, vmem_limit_bytes=56 * 2**20
        ),
        name="exchange",
    )(owned_times, hop_path, perambulators, eig, links, jnp.asarray(masks), jnp.asarray(movers))
    return pl.pallas_call(
        triple_kernel,
        grid=(slots, groups),
        out_shape=jax.ShapeDtypeStruct((slots, groups, 2, order, order), BF16),
        in_specs=[
            smem,
            smem,
            smem,
            pl.BlockSpec((1, n, 2, rows, order), lambda s, g: (s, 0, 0, 0, 0)),
            pl.BlockSpec((1, width, 2 * width), lambda s, g: (s, 0, 0)),
        ],
        out_specs=pl.BlockSpec((1, 1, 2, order, order), lambda s, g: (s, g, 0, 0, 0)),
        scratch_shapes=[
            pltpu.VMEM((order, 2 * order), BF16),
            pltpu.VMEM((order // width, 2, width, order), BF16),
        ],
        compiler_params=pltpu.CompilerParams(
            dimension_semantics=("arbitrary", "arbitrary"), vmem_limit_bytes=40 * 2**20
        ),
        name="triple",
    )(spin_perm, spin_phase, owned_times, blocks, elem)


def solution(mesh):
    in_specs = (
        P("groups", None, None, "src", None, None, None),
        P("groups", None, None, None, None, "src", None, None),
        P("groups"),
        P("groups", None),
        P("groups", None),
        P("groups", None, "src", None),
        P("groups", None),
    )
    out_specs = P(("groups", "src"), None, None, None, None)
    return jax.shard_map(
        functools.partial(shards, mesh.shape["src"]),
        mesh=mesh, in_specs=in_specs, out_specs=out_specs, check_vma=False,
    )
```

time: 78.1 us -> 82.8 us (1.060)
  Pallas kernels: 72 us -> 76.4 us
  local copies, waits for them, and re-layouts: 2.91 us -> 5.89 us
  other arithmetic: 2.27 us -> 0 us
    unnamed x8 -> x11, local copies, waits for them, and re-layouts: 0.01 us -> 5.89 us
    pallas_call x1, Pallas kernels: 63.3 us -> 67.5 us  [shards(): pl.pallas_call(functools.partial(exchange_kernel, n, hops), out_shape=(ja...]
    broadcast_in_dim x3 -> x0, local copies, waits for them, and re-layouts: 1.25 us -> none  [hop_tables(): jnp.where((hop_path < 2)[None, :, None, None, None, None], links[:, None,...]
    dynamic_slice x1 -> x0, local copies, waits for them, and re-layouts: 0.99 us -> none  [shards(): lax.dynamic_index_in_dim(owned_times, lax.axis_index('src'), 0, keepdims=...]
where the time goes in v2:
time: 82.8 us; the launch traced here: 82.3 us
  Pallas kernels  76.4 us (92%)
  local copies, waits for them, and re-layouts  5.89 us (7%)
    pallas_call x1, Pallas kernels, shards(): pl.pallas_call(functools.partial(exchange_kernel, n, hops), out_shape=(ja...  67.5 us
    pallas_call x1, Pallas kernels, shards(): pl.pallas_call(triple_kernel, grid=(slots, groups), out_shape=jax.ShapeDt...  8.83 us
    unnamed x11, local copies, waits for them, and re-layouts  5.89 us

profile of v2, /device:TPU:0, one launch (start us, length us, event | category | flops | bytes accessed | tf_op | source)
XLA Modules:
  0.0 82.3 jit_solution(4506764755779834546)
XLA Ops:
  0.0 1.4 %copy.11.owned_ref = s32[16,2]{1,0:T(8,128)} copy(s32[16,2]{0,1:T(2,128)} %param.15) | data formatting | bytes 256 | tf_op args[6]
  1.4 67.5 %exchange.1 = (bf16[2,16,2,32,512]{4,3,2,1,0:T(8,128)(2,1)}, bf16[2,128,256]{2,1,0:T(8,128)(2,1)}) custom-call(s32[16,2]{1,0:T(8,128)} %copy.11.owned_ref, s32[2]{0:T(128)} %hop_ref.1, bf16[16,2,32,512]{3,2,1,0:T(8,128)(2,1)} %pera_ref.1, bf16[16,192,128]{2,1,0:T(8,128)(2,1)} %bitcast.4, bf16[36,32,16]{2,1,0:T(8,128)(2,1)} %bitcast.5, ...), custom_call_target="tpu_custom_call" | custom-call | tf_op jit(solution)/shard_map/exchange/pallas_call | solution.py:239
  68.9 0.0 copy-start
  68.9 1.6 %copy-done = bf16[2,16,2,32,512]{4,3,2,1,0:T(8,128)(2,1)S(1)} copy-done((bf16[2,16,2,32,512]{4,3,2,1,0:T(8,128)(2,1)S(1)}, bf16[2,16,2,32,512]{4,3,2,1,0:T(8,128)(2,1)}, u32[]{:S(2)}) %copy-start) | copy-done | bytes 2097176
  70.5 0.0 copy-start.1
  70.5 0.9 %copy-done.1 = bf16[2,128,256]{2,1,0:T(8,128)(2,1)S(1)} copy-done((bf16[2,128,256]{2,1,0:T(8,128)(2,1)S(1)}, bf16[2,128,256]{2,1,0:T(8,128)(2,1)}, u32[]{:S(2)}) %copy-start.1) | copy-done | bytes 131096
  71.4 0.0 copy-start.2
  71.4 0.7 copy-done.2
  72.1 0.0 copy-start.3
  72.1 0.7 copy-done.3
  72.8 0.0 copy-start.4
  72.8 0.7 copy-done.4
  73.5 8.8 %triple.1 = bf16[2,2,2,512,512]{4,3,2,1,0:T(8,128)(2,1)} custom-call(s32[2,4]{1,0:T(2,128)S(1)} %copy-done.3, s32[2,4]{1,0:T(2,128)S(1)} %copy-done.4, s32[16,2]{1,0:T(8,128)S(1)} %copy-done.2, bf16[2,16,2,32,512]{4,3,2,1,0:T(8,128)(2,1)S(1)} %copy-done, bf16[2,128,256]{2,1,0:T(8,128)(2,1)S(1)} %copy-done.1), custom_call_target="tpu_custom_call" | custom-call | tf_op jit(solution)/shard_map/triple/pallas_call | solution.py:266
Async XLA Ops:
  68.9 1.6 %copy-start = (bf16[2,16,2,32,512]{4,3,2,1,0:T(8,128)(2,1)S(1)}, bf16[2,16,2,32,512]{4,3,2,1,0:T(8,128)(2,1)}, u32[]{:S(2)}) copy-start(bf16[2,16,2,32,512]{4,3,2,1,0:T(8,128)(2,1)} %get-tuple-element.7.blocks_ref) | copy-start | bytes 6291460
  70.5 0.9 %copy-start.1 = (bf16[2,128,256]{2,1,0:T(8,128)(2,1)S(1)}, bf16[2,128,256]{2,1,0:T(8,128)(2,1)}, u32[]{:S(2)}) copy-start(bf16[2,128,256]{2,1,0:T(8,128)(2,1)} %get-tuple-element.8.elem_ref) | copy-start | bytes 393220
  71.4 0.7 copy-start.2
  72.1 0.7 copy-start.3
  72.8 0.7 copy-start.4

commit v3 on v2

--- a/solution.py
+++ b/solution.py
@@ -30,26 +30,35 @@
 
 
 def exchange_kernel(
-    n, hops, owned_ref, hop_ref, pera_ref, eig_ref, links_ref, masks_ref, movers_ref,
+    n, hops, owned_ref, hop_ref, pera_hbm, eig_hbm, links_hbm, masks_hbm, movers_hbm,
     blocks_ref, elem_ref,
-    pstage, epart, rows_ref, hopmask, sends, recvs, keeps,
-    psend, precv, plocal, esend, erecv,
+    pera_ref, eig_ref, links_ref, masks_ref, movers_ref, fetch, pstage, epart, rows_ref, hopmask, estage, erecv, fstage, frecv,
+    psend, precv, plocal, qsend, qrecv, zsend, zrecv,
 ):
     me = lax.axis_index("src")
     slots = blocks_ref.shape[0]
     time_count = eig_ref.shape[0]
     rings = n // QUAD
-    stages = n.bit_length() - 1
     mine_q, mine_z = lax.rem(me, QUAD), me // QUAD
 
     def listed(d, s):
         return jnp.minimum(jnp.maximum(owned_ref[d, s], 0), time_count - 1)
+
+    pairs = (
+        (pera_hbm, pera_ref), (eig_hbm, eig_ref), (links_hbm, links_ref),
+        (masks_hbm, masks_ref), (movers_hbm, movers_ref),
+    )
+    fetches = [pltpu.make_async_copy(src, dst, fetch.at[i]) for i, (src, dst) in enumerate(pairs)]
+    for copy in fetches:
+        copy.start()
 
     barrier = pltpu.get_barrier_semaphore()
 
     @pl.loop(1, n)
     def _(o):
         pl.semaphore_signal(barrier, inc=1, device_id={"src": lax.rem(me + o, n)})
+
+    fetches[0].wait()
 
     @pl.loop(0, n)
     def _(d):
@@ -69,17 +78,12 @@
     def local_copy(s):
         return pltpu.make_async_copy(pstage.at[me, s], blocks_ref.at[s, me], plocal.at[s])
 
-    def send_far(s):
-        @pl.loop(0, rings - 1)
-        def _(i):
-            dz = lax.rem(i + rings // 2 - 1, rings - 1) + 1
-            for dq in range(QUAD):
-                pera_copy(dz, dq, s, False).start()
-
-    def send_near(s):
+    def send_slot(s):
         local_copy(s).start()
-        for dq in range(1, QUAD):
-            pera_copy(0, dq, s, False).start()
+
+        @pl.loop(1, n)
+        def _(o):
+            pera_copy(o // QUAD, lax.rem(o, QUAD), s, False).start()
 
     def wait_slot(s):
         @pl.loop(0, rings - 1)
@@ -91,8 +95,10 @@
             pera_copy(0, dq, s, True).wait()
         local_copy(s).wait()
 
-    send_far(0)
-
+    send_slot(0)
+
+    for copy in fetches[1:]:
+        copy.wait()
     for h in range(hops):
         code = hop_ref[h]
         pick = [(code == i).astype(F32) for i in range(4)]
@@ -131,47 +137,55 @@
             cur = jnp.concatenate([out_re, out_im], 0).astype(BF16)
         turned = jnp.concatenate([cur[half:], -cur[:half]], 0)
         both = jnp.concatenate([cur, turned], 1)
-        epart[t] = lax.dot_general(vec, both, (((0,), (0,)), ((), ())), preferred_element_type=F32)
+        part = lax.dot_general(vec, both, (((0,), (0,)), ((), ())), preferred_element_type=F32)
+        epart[t] = part.astype(BF16)
         return carry
 
     lax.fori_loop(0, time_count, one_time, 0, unroll=4)
 
+    @pl.loop(0, rings)
+    def _(z):
+        for q in range(QUAD):
+            for s in range(slots):
+                estage[q, z * slots + s] = epart[listed(z * QUAD + q, s)]
+
+    def quad_copy(o, origin):
+        peer = lax.rem(mine_q + o, QUAD)
+        return pltpu.make_async_remote_copy(
+            src_ref=estage.at[peer], dst_ref=erecv.at[origin],
+            send_sem=qsend.at[o], recv_sem=qrecv.at[o], device_id={"src": mine_z * QUAD + peer},
+        )
+
+    for o in range(1, QUAD):
+        quad_copy(o, mine_q).start()
     for s in range(1, slots):
-        send_far(s)
-
-    def elem_copy(b):
-        bit = lax.rem(me // (1 << b), 2)
+        send_slot(s)
+    for o in range(1, QUAD):
+        quad_copy(o, lax.rem(mine_q + QUAD - o, QUAD)).wait()
+
+    @pl.loop(0, rings * slots)
+    def _(j):
+        total = estage[mine_q, j].astype(F32)
+        for o in range(1, QUAD):
+            total += erecv[lax.rem(mine_q + o, QUAD), j].astype(F32)
+        fstage[j // slots, lax.rem(j, slots)] = total.astype(BF16)
+
+    def ring_copy(o, origin):
+        peer = lax.rem(mine_z + o, rings)
         return pltpu.make_async_remote_copy(
-            src_ref=sends[b], dst_ref=recvs[b], send_sem=esend.at[b], recv_sem=erecv.at[b],
-            device_id={"src": me + (1 << b) * (1 - 2 * bit)},
+            src_ref=fstage.at[peer], dst_ref=frecv.at[origin],
+            send_sem=zsend.at[o], recv_sem=zrecv.at[o], device_id={"src": peer * QUAD + mine_q},
         )
 
-    for b in range(stages):
-        bit = lax.rem(me // (1 << b), 2)
-        count = n >> (b + 1)
-
-        def value(i, s, b=b):
-            if b == 0:
-                return epart[listed(i, s)]
-            return keeps[b - 1][i, s] + recvs[b - 1][i, s].astype(F32)
-
-        @pl.loop(0, count)
-        def _(i):
-            for s in range(slots):
-                sends[b][i, s] = value(2 * i + 1 - bit, s).astype(sends[b].dtype)
-
-        elem_copy(b).start()
-
-        @pl.loop(0, count)
-        def _(i):
-            for s in range(slots):
-                keeps[b][i, s] = value(2 * i + bit, s)
-
-        elem_copy(b).wait()
-    elem_ref[...] = (keeps[stages - 1][0] + recvs[stages - 1][0].astype(F32)).astype(BF16)
-
-    for s in range(slots):
-        send_near(s)
+    for o in range(1, rings):
+        ring_copy(o, mine_z).start()
+    for o in range(1, rings):
+        ring_copy(o, lax.rem(mine_z + rings - o, rings)).wait()
+    total = fstage[mine_z].astype(F32)
+    for o in range(1, rings):
+        total += frecv[lax.rem(mine_z + o, rings)].astype(F32)
+    elem_ref[...] = total.astype(BF16)
+
     for s in range(slots):
         wait_slot(s)
 
@@ -231,38 +245,42 @@
     eig = eigenvectors.reshape(time_count, -1, width)
     links = jnp.transpose(gauge_links.reshape(time_count, 36, sites), (1, 2, 0))
     masks, movers = site_tables(side_y, side_z)
-    stages = n.bit_length() - 1
     tile = (slots, width, 2 * width)
     vmem = pl.BlockSpec(memory_space=pltpu.VMEM)
     smem = pl.BlockSpec(memory_space=pltpu.SMEM)
-    parts = [pltpu.VMEM((n >> (b + 1),) + tile, F32 if b == 0 else BF16) for b in range(stages)]
+    arrays = (perambulators, eig, links, jnp.asarray(masks), jnp.asarray(movers))
     blocks, elem = pl.pallas_call(
         functools.partial(exchange_kernel, n, hops),
         out_shape=(
             jax.ShapeDtypeStruct((slots, n, 2, rows, order), BF16),
             jax.ShapeDtypeStruct(tile, BF16),
         ),
-        in_specs=[smem, smem] + [vmem] * 5,
+        in_specs=[smem, smem] + [pl.BlockSpec(memory_space=pltpu.HBM)] * 5,
         out_specs=(pl.BlockSpec(memory_space=pl.ANY), vmem),
-        scratch_shapes=[
+        scratch_shapes=[pltpu.VMEM(a.shape, a.dtype) for a in arrays]
+        + [
+            pltpu.SemaphoreType.DMA((len(arrays),)),
             pltpu.VMEM((n, slots, 2, rows, order), BF16),
-            pltpu.VMEM((time_count, width, 2 * width), F32),
+            pltpu.VMEM((time_count, width, 2 * width), BF16),
             pltpu.VMEM((hops, 6, time_count, 3 * sites), F32),
             pltpu.VMEM((hops, sites, 3 * sites), F32),
-            parts,
-            parts,
-            [pltpu.VMEM((n >> (b + 1),) + tile, F32) for b in range(stages)],
+            pltpu.VMEM((QUAD, rings * slots, width, 2 * width), BF16),
+            pltpu.VMEM((QUAD, rings * slots, width, 2 * width), BF16),
+            pltpu.VMEM((rings,) + tile, BF16),
+            pltpu.VMEM((rings,) + tile, BF16),
             pltpu.SemaphoreType.DMA((slots, rings, QUAD)),
             pltpu.SemaphoreType.DMA((slots, rings, QUAD)),
             pltpu.SemaphoreType.DMA((slots,)),
-            pltpu.SemaphoreType.DMA((stages,)),
-            pltpu.SemaphoreType.DMA((stages,)),
+            pltpu.SemaphoreType.DMA((QUAD,)),
+            pltpu.SemaphoreType.DMA((QUAD,)),
+            pltpu.SemaphoreType.DMA((rings,)),
+            pltpu.SemaphoreType.DMA((rings,)),
         ],
         compiler_params=pltpu.CompilerParams(
             collective_id=0, has_side_effects=True, vmem_limit_bytes=56 * 2**20
         ),
         name="exchange",
-    )(owned_times, hop_path, perambulators, eig, links, jnp.asarray(masks), jnp.asarray(movers))
+    )(owned_times, hop_path, *arrays)
     return pl.pallas_call(
         triple_kernel,
         grid=(slots, groups),
@@ -280,7 +298,7 @@
             pltpu.VMEM((order // width, 2, width, order), BF16),
         ],
         compiler_params=pltpu.CompilerParams(
-            dimension_semantics=("arbitrary", "arbitrary"), vmem_limit_bytes=40 * 2**20
+            dimension_semantics=("arbitrary", "arbitrary"), vmem_limit_bytes=56 * 2**20
         ),
         name="triple",
     )(spin_perm, spin_phase, owned_times, blocks, elem)

time: 82.8 us -> 75.5 us (0.912)
  local copies, waits for them, and re-layouts: 5.89 us -> 1.35 us
  Pallas kernels: 76.4 us -> 73.5 us
    unnamed x11 -> x1, local copies, waits for them, and re-layouts: 5.89 us -> 1.35 us
    pallas_call x1, Pallas kernels: 67.5 us -> 63.9 us  [shards(): pl.pallas_call(functools.partial(exchange_kernel, n, hops), out_shape=(ja...]
where the time goes in v3:
time: 75.5 us; the launch traced here: 74.9 us
  Pallas kernels  73.5 us (97%)
  local copies, waits for them, and re-layouts  1.35 us (2%)
    pallas_call x1, Pallas kernels, shards(): pl.pallas_call(functools.partial(exchange_kernel, n, hops), out_shape=(ja...  63.9 us
    pallas_call x1, Pallas kernels, shards(): pl.pallas_call(triple_kernel, grid=(slots, groups), out_shape=jax.ShapeDt...  9.65 us

profile of v3, /device:TPU:0, one launch (start us, length us, event | category | flops | bytes accessed | tf_op | source)
XLA Modules:
  0.0 74.9 jit_solution(12943526016923210141)
XLA Ops:
  0.0 1.4 %copy.11.owned_ref = s32[16,2]{1,0:T(8,128)} copy(s32[16,2]{0,1:T(2,128)} %param.15) | data formatting | bytes 256 | tf_op args[6]
  1.4 63.9 %exchange.1 = (bf16[2,16,2,32,512]{4,3,2,1,0:T(8,128)(2,1)}, bf16[2,128,256]{2,1,0:T(8,128)(2,1)}) custom-call(s32[16,2]{1,0:T(8,128)} %copy.11.owned_ref, s32[2]{0:T(128)} %hop_ref.1, bf16[16,2,32,512]{3,2,1,0:T(8,128)(2,1)} %pera_hbm.1, bf16[16,192,128]{2,1,0:T(8,128)(2,1)} %bitcast.4, bf16[36,32,16]{2,1,0:T(8,128)(2,1)} %bitcast.5, ...), custom_call_target="tpu_custom_call" | custom-call | tf_op jit(solution)/shard_map/exchange/pallas_call | solution.py:252
  65.2 9.7 %triple.1 = bf16[2,2,2,512,512]{4,3,2,1,0:T(8,128)(2,1)} custom-call(s32[2,4]{1,0:T(2,128)} %perm_ref.1, s32[2,4]{1,0:T(2,128)} %phase_ref.1, s32[16,2]{1,0:T(8,128)} %copy.11.owned_ref, bf16[2,16,2,32,512]{4,3,2,1,0:T(8,128)(2,1)} %get-tuple-element.7.blocks_ref, bf16[2,128,256]{2,1,0:T(8,128)(2,1)} %get-tuple-element.8.elem_ref), custom_call_target="tpu_custom_call" | custom-call | tf_op jit(solution)/shard_map/triple/pallas_call | solution.py:284

commit v4 on v3

--- a/solution.py
+++ b/solution.py
@@ -42,7 +42,7 @@
     mine_q, mine_z = lax.rem(me, QUAD), me // QUAD
 
     def listed(d, s):
-        return jnp.minimum(jnp.maximum(owned_ref[d, s], 0), time_count - 1)
+        return jnp.minimum(jnp.maximum(owned_ref[s, d], 0), time_count - 1)
 
     pairs = (
         (pera_hbm, pera_ref), (eig_hbm, eig_ref), (links_hbm, links_ref),
@@ -95,7 +95,14 @@
             pera_copy(0, dq, s, True).wait()
         local_copy(s).wait()
 
-    send_slot(0)
+    for s in range(slots):
+        local_copy(s).start()
+
+    @pl.loop(1, n)
+    def _(o):
+        for s in range(slots):
+            pera_copy(o // QUAD, lax.rem(o, QUAD), s, False).start()
+
 
     for copy in fetches[1:]:
         copy.wait()
@@ -158,8 +165,6 @@
 
     for o in range(1, QUAD):
         quad_copy(o, mine_q).start()
-    for s in range(1, slots):
-        send_slot(s)
     for o in range(1, QUAD):
         quad_copy(o, lax.rem(mine_q + QUAD - o, QUAD)).wait()
 
@@ -225,7 +230,7 @@
         reals.append((scale_re * re - scale_im * im).astype(BF16))
         imags.append((scale_re * im + scale_im * re).astype(BF16))
     real, imag = jnp.concatenate(reals, 0), jnp.concatenate(imags, 0)
-    filled = owned_ref[lax.axis_index("src"), slot] >= 0
+    filled = owned_ref[slot, lax.axis_index("src")] >= 0
     lhs = left[...]
     for part, right in enumerate((jnp.concatenate([real, imag], 0), jnp.concatenate([imag, -real], 0))):
         result = jnp.dot(lhs, right, preferred_element_type=F32)
@@ -280,7 +285,7 @@
             collective_id=0, has_side_effects=True, vmem_limit_bytes=56 * 2**20
         ),
         name="exchange",
-    )(owned_times, hop_path, *arrays)
+    )(owned_times.T, hop_path, *arrays)
     return pl.pallas_call(
         triple_kernel,
         grid=(slots, groups),
@@ -301,7 +306,7 @@
             dimension_semantics=("arbitrary", "arbitrary"), vmem_limit_bytes=56 * 2**20
         ),
         name="triple",
-    )(spin_perm, spin_phase, owned_times, blocks, elem)
+    )(spin_perm, spin_phase, owned_times.T, blocks, elem)
 
 
 def solution(mesh):

time: 75.5 us -> 73.9 us (0.979)
  local copies, waits for them, and re-layouts: 1.35 us -> 0 us
    unnamed x1 -> x0, local copies, waits for them, and re-layouts: 1.35 us -> none
where the time goes in v4:
time: 73.9 us; the launch traced here: 73.4 us
  Pallas kernels  73.4 us (99%)
    pallas_call x1, Pallas kernels, shards(): pl.pallas_call(functools.partial(exchange_kernel, n, hops), out_shape=(ja...  63.7 us
    pallas_call x1, Pallas kernels, shards(): pl.pallas_call(triple_kernel, grid=(slots, groups), out_shape=jax.ShapeDt...  9.65 us

profile of v4, /device:TPU:0, one launch (start us, length us, event | category | flops | bytes accessed | tf_op | source)
XLA Modules:
  0.0 73.4 jit_solution(12999045258957007981)
XLA Ops:
  0.0 63.7 %exchange.1 = (bf16[2,16,2,32,512]{4,3,2,1,0:T(8,128)(2,1)}, bf16[2,128,256]{2,1,0:T(8,128)(2,1)}) custom-call(s32[2,16]{1,0:T(2,128)} %bitcast.7, s32[2]{0:T(128)} %hop_ref.1, bf16[16,2,32,512]{3,2,1,0:T(8,128)(2,1)} %pera_hbm.1, bf16[16,192,128]{2,1,0:T(8,128)(2,1)} %bitcast.5, bf16[36,32,16]{2,1,0:T(8,128)(2,1)} %bitcast.6, ...), custom_call_target="tpu_custom_call" | custom-call | tf_op jit(solution)/shard_map/exchange/pallas_call | solution.py:257
  63.7 9.6 %triple.1 = bf16[2,2,2,512,512]{4,3,2,1,0:T(8,128)(2,1)} custom-call(s32[2,4]{1,0:T(2,128)} %perm_ref.1, s32[2,4]{1,0:T(2,128)} %phase_ref.1, s32[2,16]{1,0:T(2,128)} %bitcast.8, bf16[2,16,2,32,512]{4,3,2,1,0:T(8,128)(2,1)} %get-tuple-element.7.blocks_ref, bf16[2,128,256]{2,1,0:T(8,128)(2,1)} %get-tuple-element.8.elem_ref), custom_call_target="tpu_custom_call" | custom-call | tf_op jit(solution)/shard_map/triple/pallas_call | solution.py:289
